TPU v7x, 32 devices: a whole 2x2x4 slice. The times are simulated.
32 devices in a mesh: tm: 4 (over x, core), chan: 8 (over z, y).
Axes of the slice: x: 2, y: 2, z: 4, core: 2. Of those that a mesh axis runs over, the one named last changes fastest.
Arguments:
- samples: bfloat16 [384, 128], P('chan', 'tm'), may hold values from -6 to 6
- dead_channels: int32 [12], replicated, may hold values from 0 to 383
- first_kernel: bfloat16 [8, 32], replicated, may hold values from -3 to 3
- dilated_one: bfloat16 [3, 32, 64], replicated, may hold values from -0.875 to 0.875
- dilated_two: bfloat16 [3, 64, 128], replicated, may hold values from -0.625 to 0.625
- dilated_three: bfloat16 [3, 128, 256], replicated, may hold values from -0.4375 to 0.4375
- dilated_four: bfloat16 [3, 256, 256], replicated, may hold values from -0.3125 to 0.3125
- embed_weight: bfloat16 [256, 512], replicated, may hold values from -0.375 to 0.375
- gain_one: float32 [512], replicated, may hold values from 0.1 to 1.9
- project_in: bfloat16 [512, 1536], replicated, may hold values from -1 to 1
- project_out: bfloat16 [512, 512], replicated, may hold values from -0.25 to 0.25
- gain_two: float32 [512], replicated, may hold values from 0.1 to 1.9
- up_weight: bfloat16 [512, 2048], replicated, may hold values from -0.25 to 0.25
- down_weight: bfloat16 [2048, 512], replicated, may hold values from -0.125 to 0.125
Outputs:
- encoded: bfloat16 [32, 384, 512], P('tm', 'chan')
Inputs may be any that keep to these rules, and one draw needn't show every extreme that they name: `dead_channels`: channel numbers; a number may repeat.
All inputs are finite; a program needn't handle non-finite values.
Results may differ from a plain program's by a relative error of at most 0.015.
Values may be sent and summed in bfloat16 or wider, within the bound.
A program may use at most 64 MiB of HBM per device.

v0:
```python
import jax
import jax.numpy as jnp
from jax import lax
from jax.sharding import PartitionSpec as P

HEADS = 8
KERNEL = 8
STRIDE = 4
EPSILON = 1e-05
DILATIONS = (1, 2, 4, 8)


def extended_2(cells, sides, width):
    for axis, dim in sides:
        count = lax.axis_size(axis)
        ends = count - 1
        head = lax.slice_in_dim(cells, 0, width, axis=dim)
        tail = lax.slice_in_dim(cells, cells.shape[dim] - width, cells.shape[dim], axis=dim)
        cells = jnp.concatenate(
            [
                lax.ppermute(tail, axis, [(i, (i + 1) % count) for i in range(ends)]),
                cells,
                lax.ppermute(head, axis, [((i + 1) % count, i) for i in range(ends)]),
            ],
            axis=dim,
        )
    return cells


def normalize(tokens, gain):
    floats = tokens.astype(jnp.float32)
    average = jnp.mean(floats, axis=-1, keepdims=True)
    centred = floats - average
    variance = jnp.mean(centred * centred, axis=-1, keepdims=True)
    return (centred * lax.rsqrt(variance + EPSILON) * gain).astype(jnp.bfloat16)


def attend(query_rows, key_rows, value_rows, alive_mask):
    count = query_rows.shape[0]
    block_rows = min(512, count)
    scaling = query_rows.shape[2] ** (-0.5)

    def one_head(operands):
        queries, keys_head, values_head = operands
        blocks = queries.reshape(count // block_rows, block_rows, queries.shape[1])

        def one_block(query_block):
            scores = jnp.dot(query_block, keys_head.T, preferred_element_type=jnp.float32) * scaling
            scores = jnp.where(alive_mask[None, :], scores, -1e30)
            largest = jnp.max(scores, axis=1, keepdims=True)
            exponent = jnp.exp(scores - largest)
            weights = (exponent / jnp.sum(exponent, axis=1, keepdims=True)).astype(jnp.bfloat16)
            return jnp.dot(weights, values_head, preferred_element_type=jnp.float32).astype(
                jnp.bfloat16
            )

        return lax.map(one_block, blocks).reshape(count, queries.shape[1])

    heads_first = lax.map(
        one_head,
        (
            jnp.swapaxes(query_rows, 0, 1),
            jnp.swapaxes(key_rows, 0, 1),
            jnp.swapaxes(value_rows, 0, 1),
        ),
    )
    return jnp.swapaxes(heads_first, 0, 1).reshape(count, -1)


def encoder(
    embedded, alive_mask, gain_one, project_in, project_out, gain_two, up_weight, down_weight
):
    count, width = embedded.shape
    normed = normalize(embedded, gain_one)
    projected = jnp.dot(normed, project_in, preferred_element_type=jnp.float32).astype(jnp.bfloat16)
    pieces = projected.reshape(count, 3, HEADS, width // HEADS)
    attended = attend(pieces[:, 0], pieces[:, 1], pieces[:, 2], alive_mask)
    mixed = (
        embedded.astype(jnp.float32)
        + jnp.dot(attended, project_out, preferred_element_type=jnp.float32)
    ).astype(jnp.bfloat16)
    normed_two = normalize(mixed, gain_two)
    inner = jax.nn.gelu(jnp.dot(normed_two, up_weight, preferred_element_type=jnp.float32)).astype(
        jnp.bfloat16
    )
    return (
        mixed.astype(jnp.float32) + jnp.dot(inner, down_weight, preferred_element_type=jnp.float32)
    ).astype(jnp.bfloat16)


def patch_conv(padded, first_kernel, frames):
    taps = jnp.stack(
        [
            padded[:, offset : offset + STRIDE * (frames - 1) + 1 : STRIDE]
            for offset in range(KERNEL)
        ],
        axis=-1,
    )
    summed = jnp.einsum("cfk,ko->fco", taps, first_kernel, preferred_element_type=jnp.float32)
    return jax.nn.gelu(summed).astype(jnp.bfloat16)


def dilated(padded, weight, dilation, frames):
    summed = jnp.zeros((frames, padded.shape[1], weight.shape[2]), jnp.float32)
    for offset in range(3):
        window = padded[offset * dilation : offset * dilation + frames]
        summed = summed + jnp.einsum(
            "fci,io->fco", window, weight[offset], preferred_element_type=jnp.float32
        )
    return jax.nn.gelu(summed).astype(jnp.bfloat16)


def project_rows(features, embed_weight):
    return jnp.einsum(
        "fci,io->fco", features, embed_weight, preferred_element_type=jnp.float32
    ).astype(jnp.bfloat16)


def per_device(
    samples,
    dead_channels,
    first_kernel,
    dilated_one,
    dilated_two,
    dilated_three,
    dilated_four,
    embed_weight,
    gain_one,
    project_in,
    project_out,
    gain_two,
    up_weight,
    down_weight,
):
    channels_dev, sample_count = samples.shape
    groups = lax.axis_size("chan")
    channel_total = channels_dev * groups
    own_ids = lax.axis_index("chan") * channels_dev + jnp.arange(channels_dev, dtype=jnp.int32)
    own_alive = jnp.logical_not(jnp.any(own_ids[:, None] == dead_channels[None, :], axis=1))
    signal = jnp.where(own_alive[:, None], samples, jnp.zeros_like(samples))
    rim_width = (KERNEL - STRIDE) // 2
    weights_list = (dilated_one, dilated_two, dilated_three, dilated_four)
    padded = extended_2(signal, (("tm", 1),), rim_width)
    frames = sample_count // STRIDE
    hidden = patch_conv(padded, first_kernel, frames)
    for weight, dilation in zip(weights_list, DILATIONS):
        extended = extended_2(hidden, (("tm", 0),), dilation)
        hidden = dilated(extended, weight, dilation, frames)
    embedded = project_rows(hidden, embed_weight)
    embedded = lax.all_to_all(embedded, "chan", split_axis=0, concat_axis=1, tiled=True)
    all_ids = jnp.arange(channel_total, dtype=jnp.int32)
    alive_mask = jnp.logical_not(jnp.any(all_ids[:, None] == dead_channels[None, :], axis=1))

    def per_frame(frame_tokens):
        return encoder(
            frame_tokens,
            alive_mask,
            gain_one,
            project_in,
            project_out,
            gain_two,
            up_weight,
            down_weight,
        )

    result = lax.map(per_frame, embedded)
    return lax.all_to_all(result, "chan", split_axis=1, concat_axis=0, tiled=True)


def solution(mesh):
    return jax.shard_map(
        per_device,
        mesh=mesh,
        in_specs=(P("chan", "tm"), P(), P(), P(), P(), P(), P(), P(), P(), P(), P(), P(), P(), P()),
        out_specs=P("tm", "chan", None),
        check_vma=False,
    )
```

profile of v0, /device:TPU:0, one launch (start us, length us, event | category | flops | bytes accessed | tf_op | source)
XLA Modules:
  0.0 116.4 jit_solution(12862702731849805293)
XLA Ops:
  1.6 2.4 %collective-permute-start = (bf16[48,2]{0,1:T(2,128)(2,1)S(1)}, bf16[48,2]{0,1:T(2,128)(2,1)S(1)}, u32[]{:S(2)}, u32[]{:S(2)}) collective-permute-start(bf16[48,2]{0,1:T(2,128)(2,1)S(1)} %get-tuple-element.175), channel_id=1, source_target_pairs={{0,8},{8,16},{16,24},{1,9},{9,17},{17,25},{2,10},{10,18},{18,26},{... | collective-permute-start | bytes 584 | tf_op jit(solution)/shard_map/ppermute | solution.py:21
  4.0 1.3 %collective-permute-start.1 = (bf16[48,2]{0,1:T(2,128)(2,1)S(1)}, bf16[48,2]{0,1:T(2,128)(2,1)S(1)}, u32[]{:S(2)}, u32[]{:S(2)}) collective-permute-start(bf16[48,2]{0,1:T(2,128)(2,1)S(1)} %get-tuple-element.176), channel_id=1, source_target_pairs={{8,0},{16,8},{24,16},{9,1},{17,9},{25,17},{10,2},{18,10},{26,18},{... | collective-permute-start | bytes 584 | tf_op jit(solution)/shard_map/ppermute | solution.py:23
  5.5 3.7 %collective-permute-done.1 = bf16[48,2]{0,1:T(2,128)(2,1)S(1)} collective-permute-done((bf16[48,2]{0,1:T(2,128)(2,1)S(1)}, bf16[48,2]{0,1:T(2,128)(2,1)S(1)}, u32[]{:S(2)}, u32[]{:S(2)}) %collective-permute-start.1) | collective-permute-done | bytes 224 | tf_op jit(solution)/shard_map/ppermute | solution.py:23
  10.3 1.3 %collective-permute-start.3 = (bf16[1,48,32]{1,2,0:T(8,128)(2,1)S(1)}, bf16[1,48,32]{1,2,0:T(8,128)(2,1)S(1)}, u32[]{:S(2)}, u32[]{:S(2)}) collective-permute-start(bf16[1,48,32]{1,2,0:T(8,128)(2,1)S(1)} %get-tuple-element.174), channel_id=1, source_target_pairs={{8,0},{16,8},{24,16},{9,1},{17,9},{25,17},{10,2},{18,10},{26,18},{... | collective-permute-start | bytes 9224 | tf_op jit(solution)/shard_map/ppermute | solution.py:23
  11.6 4.9 %collective-permute-start.2 = (bf16[1,48,32]{1,2,0:T(8,128)(2,1)S(1)}, bf16[1,48,32]{1,2,0:T(8,128)(2,1)S(1)}, u32[]{:S(2)}, u32[]{:S(2)}) collective-permute-start(bf16[1,48,32]{1,2,0:T(8,128)(2,1)S(1)} %get-tuple-element.173), channel_id=1, source_target_pairs={{0,8},{8,16},{16,24},{1,9},{9,17},{17,25},{2,10},{10,18},{18,26},{... | collective-permute-start | bytes 9224 | tf_op jit(solution)/shard_map/ppermute | solution.py:21
  18.3 1.0 fusion.71
  19.3 1.4 %collective-permute-start.5 = (bf16[2,48,64]{2,1,0:T(8,128)(2,1)S(1)}, bf16[2,48,64]{2,1,0:T(8,128)(2,1)S(1)}, u32[]{:S(2)}, u32[]{:S(2)}) collective-permute-start(bf16[2,48,64]{2,1,0:T(8,128)(2,1)S(1)} %get-tuple-element.172), channel_id=1, source_target_pairs={{8,0},{16,8},{24,16},{9,1},{17,9},{25,17},{10,2},{18,10},{26,18},{... | collective-permute-start | bytes 36872 | tf_op jit(solution)/shard_map/ppermute | solution.py:23
  21.6 4.3 %collective-permute-start.4 = (bf16[2,48,64]{2,1,0:T(8,128)(2,1)S(1)}, bf16[2,48,64]{2,1,0:T(8,128)(2,1)S(1)}, u32[]{:S(2)}, u32[]{:S(2)}) collective-permute-start(bf16[2,48,64]{2,1,0:T(8,128)(2,1)S(1)} %get-tuple-element.171), channel_id=1, source_target_pairs={{0,8},{8,16},{16,24},{1,9},{9,17},{17,25},{2,10},{10,18},{18,26},{... | collective-permute-start | bytes 36872 | tf_op jit(solution)/shard_map/ppermute | solution.py:21
  27.0 1.4 %collective-permute-start.7 = (bf16[4,48,128]{2,1,0:T(8,128)(2,1)S(1)}, bf16[4,48,128]{2,1,0:T(8,128)(2,1)S(1)}, u32[]{:S(2)}, u32[]{:S(2)}) collective-permute-start(bf16[4,48,128]{2,1,0:T(8,128)(2,1)S(1)} %get-tuple-element.170), channel_id=1, source_target_pairs={{8,0},{16,8},{24,16},{9,1},{17,9},{25,17},{10,2},{18,10},{26,18},{... | collective-permute-start | bytes 147464 | tf_op jit(solution)/shard_map/ppermute | solution.py:23
  28.6 4.4 %collective-permute-start.6 = (bf16[4,48,128]{2,1,0:T(8,128)(2,1)S(1)}, bf16[4,48,128]{2,1,0:T(8,128)(2,1)S(1)}, u32[]{:S(2)}, u32[]{:S(2)}) collective-permute-start(bf16[4,48,128]{2,1,0:T(8,128)(2,1)S(1)} %get-tuple-element.169), channel_id=1, source_target_pairs={{0,8},{8,16},{16,24},{1,9},{9,17},{17,25},{2,10},{10,18},{18,26},{... | collective-permute-start | bytes 147464 | tf_op jit(solution)/shard_map/ppermute | solution.py:21
  34.2 1.3 %collective-permute-start.9 = (bf16[8,48,256]{2,1,0:T(8,128)(2,1)S(1)}, bf16[8,48,256]{2,1,0:T(8,128)(2,1)S(1)}, u32[]{:S(2)}, u32[]{:S(2)}) collective-permute-start(bf16[8,48,256]{2,1,0:T(8,128)(2,1)S(1)} %fusion.47), channel_id=1, source_target_pairs={{8,0},{16,8},{24,16},{9,1},{17,9},{25,17},{10,2},{18,10},{26,18},{... | collective-permute-start | bytes 589832 | tf_op jit(solution)/shard_map/ppermute | solution.py:23
  35.5 5.8 %collective-permute-start.8 = (bf16[8,48,256]{2,1,0:T(8,128)(2,1)S(1)}, bf16[8,48,256]{2,1,0:T(8,128)(2,1)}, u32[]{:S(2)}, u32[]{:S(2)}) collective-permute-start(bf16[8,48,256]{2,1,0:T(8,128)(2,1)S(1)} %fusion.47), channel_id=1, source_target_pairs={{0,8},{8,16},{16,24},{1,9},{9,17},{17,25},{2,10},{10,18},{18,26},{... | collective-permute-start | bytes 589832 | tf_op jit(solution)/shard_map/ppermute | solution.py:21
  41.8 2.1 %convolution_convert_fusion.2 = bf16[8,48,512]{2,1,0:T(8,128)(2,1)} fusion(f32[8,48,256]{2,1,0:T(8,128)S(1)} %fusion.99, f32[8,48,256]{2,1,0:T(8,128)S(1)} %fusion.101, bf16[8,48,256]{2,1,0:T(8,128)(2,1)} %collective-permute-done.8, bf16[256,512]{1,0:T(8,128)(2,1)S(1)} %copy-done.5, bf16[3,256,256]{2,1,0:T(8,128)(2,1)S(1)} %copy-done.1), kind=kOutput, calls=%fused_computation.32 | convolution fusion | flops 152272896 | bytes 1769472 | tf_op jit(solution)/shard_map/fci,io->fco/dot_general | solution.py:114
  43.9 5.8 %all-to-all-start = ((bf16[8,48,512]{2,1,0:T(8,128)(2,1)}), bf16[8,48,512]{2,1,0:T(8,128)(2,1)S(1)}, u32[]{:S(2)}, u32[]{:S(2)}) async-start(bf16[8,48,512]{2,1,0:T(8,128)(2,1)} %convolution_convert_fusion.2), calls=%async_computation | async-start | bytes 786432 | tf_op jit(solution)/shard_map/all_to_all | solution.py:150
  49.9 9.2 %all-to-all-done = bf16[8,48,512]{2,1,0:T(8,128)(2,1)S(1)} async-done(((bf16[8,48,512]{2,1,0:T(8,128)(2,1)}), bf16[8,48,512]{2,1,0:T(8,128)(2,1)S(1)}, u32[]{:S(2)}, u32[]{:S(2)}) %all-to-all-start) | async-done | bytes 393248 | tf_op jit(solution)/shard_map/all_to_all | solution.py:150
  59.8 3.2 %convolution_convert_fusion.1 = bf16[384,1536]{1,0:T(8,128)(2,1)} fusion(bf16[384,512]{1,0:T(8,128)(2,1)S(1)} %fusion.39, bf16[512,1536]{1,0:T(8,128)(2,1)} %param.25), kind=kOutput, calls=%fused_computation.25 | convolution fusion | flops 604569600 | bytes 3145728 | tf_op jit(solution)/shard_map/while/body/eval_jaxpr/dot_general | solution.py:75
  63.1 2.4 %copy.148 = bf16[384,1536]{0,1:T(8,128)(2,1)} copy(bf16[384,1536]{1,0:T(8,128)(2,1)} %convolution_convert_fusion.1) | data formatting | bytes 2359296 | tf_op jit(solution)/shard_map/while/body/eval_jaxpr/convert_element_type | solution.py:75
  65.4 2.1 %slice_bitcast_fusion = (bf16[8,384,64]{1,2,0:T(8,128)(2,1)}, bf16[8,384,64]{1,2,0:T(8,128)(2,1)S(1)}, bf16[8,384,64]{1,2,0:T(8,128)(2,1)S(1)}) fusion(bf16[384,3,8,64]{0,3,2,1:T(8,128)(2,1)} %bitcast.143), kind=kLoop, calls=%fused_computation.70 | loop fusion | bytes 2359296 | tf_op jit(solution)/shard_map/while/body/eval_jaxpr/transpose | solution.py:64
  67.6 16.7 %while.17 = (s32[]{:T(128)}, bf16[8,384,64]{1,2,0:T(8,128)(2,1)}, pred[384]{0:T(512)(128)(4,1)S(1)}, bf16[8,384,64]{1,2,0:T(8,128)(2,1)S(1)}, bf16[8,384,64]{1,2...) while((s32[]{:T(128)}, bf16[8,384,64]{1,2,0:T(8,128)(2,1)}, pred[384]{0:T(512)(128)(4,1)S(1)}, ...), condition=%wide.region_7.8_spmd, body=%wide.region_4.7_spmd.sunk | while | flops 38952192 | bytes 1976397 | solution.py:59
  68.0 1.7 %fusion.186 = bf16[8,384,64]{1,2,0:T(8,128)(2,1)} fusion(bf16[8,384,64]{1,2,0:T(8,128)(2,1)} %get-tuple-element.228, s32[]{:T(128)} %get-tuple-element.227, f32[384,384]{0,1:T(8,128)S(1)} %get-tuple-element.218, f32[384]{0:T(512)S(1)} %fusion.185, f32[384]{0:T(512)S(1)} %get-tuple-element.219, bf16[8,384,64]{1,2,0:T(8,128)(2,1)} %get-tuple-element.239), kind=kOutput, calls=%fused_computation.4.clone.1 | convolution fusion | flops 19341312 | bytes 692224 | tf_op jit(solution)/shard_map/while/body/eval_jaxpr/while/body/eval_jaxpr/while/body/eval_jaxpr/dot_general | solution.py:53
  70.1 1.7 %fusion.186 = bf16[8,384,64]{1,2,0:T(8,128)(2,1)} fusion(bf16[8,384,64]{1,2,0:T(8,128)(2,1)} %get-tuple-element.228, s32[]{:T(128)} %get-tuple-element.227, f32[384,384]{0,1:T(8,128)S(1)} %get-tuple-element.218, f32[384]{0:T(512)S(1)} %fusion.185, f32[384]{0:T(512)S(1)} %get-tuple-element.219, bf16[8,384,64]{1,2,0:T(8,128)(2,1)} %get-tuple-element.239), kind=kOutput, calls=%fused_computation.4.clone.1 | convolution fusion | flops 19341312 | bytes 692224 | tf_op jit(solution)/shard_map/while/body/eval_jaxpr/while/body/eval_jaxpr/while/body/eval_jaxpr/dot_general | solution.py:53
  72.2 1.7 %fusion.186 = bf16[8,384,64]{1,2,0:T(8,128)(2,1)} fusion(bf16[8,384,64]{1,2,0:T(8,128)(2,1)} %get-tuple-element.228, s32[]{:T(128)} %get-tuple-element.227, f32[384,384]{0,1:T(8,128)S(1)} %get-tuple-element.218, f32[384]{0:T(512)S(1)} %fusion.185, f32[384]{0:T(512)S(1)} %get-tuple-element.219, bf16[8,384,64]{1,2,0:T(8,128)(2,1)} %get-tuple-element.239), kind=kOutput, calls=%fused_computation.4.clone.1 | convolution fusion | flops 19341312 | bytes 692224 | tf_op jit(solution)/shard_map/while/body/eval_jaxpr/while/body/eval_jaxpr/while/body/eval_jaxpr/dot_general | solution.py:53
  74.3 1.7 %fusion.186 = bf16[8,384,64]{1,2,0:T(8,128)(2,1)} fusion(bf16[8,384,64]{1,2,0:T(8,128)(2,1)} %get-tuple-element.228, s32[]{:T(128)} %get-tuple-element.227, f32[384,384]{0,1:T(8,128)S(1)} %get-tuple-element.218, f32[384]{0:T(512)S(1)} %fusion.185, f32[384]{0:T(512)S(1)} %get-tuple-element.219, bf16[8,384,64]{1,2,0:T(8,128)(2,1)} %get-tuple-element.239), kind=kOutput, calls=%fused_computation.4.clone.1 | convolution fusion | flops 19341312 | bytes 692224 | tf_op jit(solution)/shard_map/while/body/eval_jaxpr/while/body/eval_jaxpr/while/body/eval_jaxpr/dot_general | solution.py:53
  76.3 1.7 %fusion.186 = bf16[8,384,64]{1,2,0:T(8,128)(2,1)} fusion(bf16[8,384,64]{1,2,0:T(8,128)(2,1)} %get-tuple-element.228, s32[]{:T(128)} %get-tuple-element.227, f32[384,384]{0,1:T(8,128)S(1)} %get-tuple-element.218, f32[384]{0:T(512)S(1)} %fusion.185, f32[384]{0:T(512)S(1)} %get-tuple-element.219, bf16[8,384,64]{1,2,0:T(8,128)(2,1)} %get-tuple-element.239), kind=kOutput, calls=%fused_computation.4.clone.1 | convolution fusion | flops 19341312 | bytes 692224 | tf_op jit(solution)/shard_map/while/body/eval_jaxpr/while/body/eval_jaxpr/while/body/eval_jaxpr/dot_general | solution.py:53
  78.4 1.7 %fusion.186 = bf16[8,384,64]{1,2,0:T(8,128)(2,1)} fusion(bf16[8,384,64]{1,2,0:T(8,128)(2,1)} %get-tuple-element.228, s32[]{:T(128)} %get-tuple-element.227, f32[384,384]{0,1:T(8,128)S(1)} %get-tuple-element.218, f32[384]{0:T(512)S(1)} %fusion.185, f32[384]{0:T(512)S(1)} %get-tuple-element.219, bf16[8,384,64]{1,2,0:T(8,128)(2,1)} %get-tuple-element.239), kind=kOutput, calls=%fused_computation.4.clone.1 | convolution fusion | flops 19341312 | bytes 692224 | tf_op jit(solution)/shard_map/while/body/eval_jaxpr/while/body/eval_jaxpr/while/body/eval_jaxpr/dot_general | solution.py:53
  80.5 1.7 %fusion.186 = bf16[8,384,64]{1,2,0:T(8,128)(2,1)} fusion(bf16[8,384,64]{1,2,0:T(8,128)(2,1)} %get-tuple-element.228, s32[]{:T(128)} %get-tuple-element.227, f32[384,384]{0,1:T(8,128)S(1)} %get-tuple-element.218, f32[384]{0:T(512)S(1)} %fusion.185, f32[384]{0:T(512)S(1)} %get-tuple-element.219, bf16[8,384,64]{1,2,0:T(8,128)(2,1)} %get-tuple-element.239), kind=kOutput, calls=%fused_computation.4.clone.1 | convolution fusion | flops 19341312 | bytes 692224 | tf_op jit(solution)/shard_map/while/body/eval_jaxpr/while/body/eval_jaxpr/while/body/eval_jaxpr/dot_general | solution.py:53
  82.6 1.7 %fusion.186 = bf16[8,384,64]{1,2,0:T(8,128)(2,1)} fusion(bf16[8,384,64]{1,2,0:T(8,128)(2,1)} %get-tuple-element.228, s32[]{:T(128)} %get-tuple-element.227, f32[384,384]{0,1:T(8,128)S(1)} %get-tuple-element.218, f32[384]{0:T(512)S(1)} %fusion.185, f32[384]{0:T(512)S(1)} %get-tuple-element.219, bf16[8,384,64]{1,2,0:T(8,128)(2,1)} %get-tuple-element.239), kind=kOutput, calls=%fused_computation.4.clone.1 | convolution fusion | flops 19341312 | bytes 692224 | tf_op jit(solution)/shard_map/while/body/eval_jaxpr/while/body/eval_jaxpr/while/body/eval_jaxpr/dot_general | solution.py:53
  84.3 1.7 %fusion.165 = (f32[384]{0:T(512)S(1)}, f32[384,512]{1,0:T(8,128)S(1)}) fusion(bf16[384,512]{0,1:T(8,128)(2,1)} %bitcast.146, bf16[512,512]{1,0:T(8,128)(2,1)} %param.26, bf16[384,512]{1,0:T(8,128)(2,1)S(1)} %bitcast.142), kind=kOutput, calls=%fused_computation.188 | convolution fusion | flops 202309248 | bytes 2098688 | tf_op jit(solution)/shard_map/while/body/eval_jaxpr/dot_general | solution.py:80
  86.2 4.4 %fusion.30 = bf16[1,384,512]{2,1,0:T(8,128)(2,1)} fusion(f32[384,512]{1,0:T(8,128)S(1)} %get-tuple-element.178, bf16[2048,512]{1,0:T(8,128)(2,1)S(1)} %copy-done, bf16[512,2048]{1,0:T(8,128)(2,1)} %param.28, f32[512]{0:T(512)S(1)} %copy-done.6, f32[384]{0:T(512)S(1)} %add_rsqrt_fusion.1, f32[384]{0:T(512)S(1)} %broadcast_multiply_fusion.1), kind=kOutput, calls=%fused_computation.33 | convolution fusion | flops 1618870272 | bytes 5379072 | tf_op jit(solution)/shard_map/while/body/eval_jaxpr/dot_general | solution.py:87
  90.6 1.6 %copy.158 = bf16[1,384,512]{2,0,1:T(2,128)(2,1)S(1)} copy(bf16[1,384,512]{2,1,0:T(8,128)(2,1)} %fusion.30) | data formatting | bytes 786432 | tf_op jit(solution)/shard_map/while/body/jit(dynamic_update_index_in_dim)/broadcast_in_dim | solution.py:166
  92.7 3.0 %reduce.8 = bf16[384,512]{1,0:T(8,128)(2,1)S(1)} reduce(bf16[384,1,512]{2,1,0:T(2,128)(2,1)S(1)} %bitcast.144, bf16[]{:T(256)} %broadcast.175), dimensions={1}, to_apply=%bitcast.133.reduce_sub_computation | reduce | bytes 786434
  96.0 19.2 %all_to_all.21 = bf16[8,2,12288]{2,1,0:T(2,128)(2,1)S(1)} all-to-all(bf16[8,2,12288]{2,1,0:T(2,128)(2,1)S(1)} %reshape.104), channel_id=1, replica_groups=mesh['tm'=4,'chan'=8] {'chan'}, dimensions={0} | all-to-all | bytes 786432 | tf_op jit(solution)/shard_map/all_to_all | solution.py:167
  (95 shorter events, 15.0 us)
Async XLA Ops:
  0.0 86.2 %copy-start = (bf16[2048,512]{1,0:T(8,128)(2,1)S(1)}, bf16[2048,512]{1,0:T(8,128)(2,1)}, u32[]{:S(2)}) copy-start(bf16[2048,512]{1,0:T(8,128)(2,1)} %param.29) | copy-start | bytes 6291460
  0.0 25.9 %copy-start.3 = (bf16[3,64,128]{2,1,0:T(8,128)(2,1)S(1)}, bf16[3,64,128]{2,1,0:T(8,128)(2,1)}, u32[]{:S(2)}) copy-start(bf16[3,64,128]{2,1,0:T(8,128)(2,1)} %param.20) | copy-start | bytes 147460
  0.0 28.4 %copy-start.2 = (bf16[3,128,256]{2,1,0:T(8,128)(2,1)S(1)}, bf16[3,128,256]{2,1,0:T(8,128)(2,1)}, u32[]{:S(2)}) copy-start(bf16[3,128,256]{2,1,0:T(8,128)(2,1)} %param.21) | copy-start | bytes 589828
  1.6 3.8 %collective-permute-start = (bf16[48,2]{0,1:T(2,128)(2,1)S(1)}, bf16[48,2]{0,1:T(2,128)(2,1)S(1)}, u32[]{:S(2)}, u32[]{:S(2)}) collective-permute-start(bf16[48,2]{0,1:T(2,128)(2,1)S(1)} %get-tuple-element.175), channel_id=1, source_target_pairs={{0,8},{8,16},{16,24},{1,9},{9,17},{17,25},{2,10},{10,18},{18,26},{... | collective-permute-start | bytes 584 | tf_op jit(solution)/shard_map/ppermute | solution.py:21
  4.0 5.1 %collective-permute-start.1 = (bf16[48,2]{0,1:T(2,128)(2,1)S(1)}, bf16[48,2]{0,1:T(2,128)(2,1)S(1)}, u32[]{:S(2)}, u32[]{:S(2)}) collective-permute-start(bf16[48,2]{0,1:T(2,128)(2,1)S(1)} %get-tuple-element.176), channel_id=1, source_target_pairs={{8,0},{16,8},{24,16},{9,1},{17,9},{25,17},{10,2},{18,10},{26,18},{... | collective-permute-start | bytes 584 | tf_op jit(solution)/shard_map/ppermute | solution.py:23
  10.3 7.1 %collective-permute-start.3 = (bf16[1,48,32]{1,2,0:T(8,128)(2,1)S(1)}, bf16[1,48,32]{1,2,0:T(8,128)(2,1)S(1)}, u32[]{:S(2)}, u32[]{:S(2)}) collective-permute-start(bf16[1,48,32]{1,2,0:T(8,128)(2,1)S(1)} %get-tuple-element.174), channel_id=1, source_target_pairs={{8,0},{16,8},{24,16},{9,1},{17,9},{25,17},{10,2},{18,10},{26,18},{... | collective-permute-start | bytes 9224 | tf_op jit(solution)/shard_map/ppermute | solution.py:23
  11.6 6.7 %collective-permute-start.2 = (bf16[1,48,32]{1,2,0:T(8,128)(2,1)S(1)}, bf16[1,48,32]{1,2,0:T(8,128)(2,1)S(1)}, u32[]{:S(2)}, u32[]{:S(2)}) collective-permute-start(bf16[1,48,32]{1,2,0:T(8,128)(2,1)S(1)} %get-tuple-element.173), channel_id=1, source_target_pairs={{0,8},{8,16},{16,24},{1,9},{9,17},{17,25},{2,10},{10,18},{18,26},{... | collective-permute-start | bytes 9224 | tf_op jit(solution)/shard_map/ppermute | solution.py:21
  19.3 22.0 %copy-start.1 = (bf16[3,256,256]{2,1,0:T(8,128)(2,1)S(1)}, bf16[3,256,256]{2,1,0:T(8,128)(2,1)}, u32[]{:S(2)}) copy-start(bf16[3,256,256]{2,1,0:T(8,128)(2,1)} %param.22) | copy-start | bytes 1179652
  19.3 6.6 %collective-permute-start.5 = (bf16[2,48,64]{2,1,0:T(8,128)(2,1)S(1)}, bf16[2,48,64]{2,1,0:T(8,128)(2,1)S(1)}, u32[]{:S(2)}, u32[]{:S(2)}) collective-permute-start(bf16[2,48,64]{2,1,0:T(8,128)(2,1)S(1)} %get-tuple-element.172), channel_id=1, source_target_pairs={{8,0},{16,8},{24,16},{9,1},{17,9},{25,17},{10,2},{18,10},{26,18},{... | collective-permute-start | bytes 36872 | tf_op jit(solution)/shard_map/ppermute | solution.py:23
  21.6 5.1 %collective-permute-start.4 = (bf16[2,48,64]{2,1,0:T(8,128)(2,1)S(1)}, bf16[2,48,64]{2,1,0:T(8,128)(2,1)S(1)}, u32[]{:S(2)}, u32[]{:S(2)}) collective-permute-start(bf16[2,48,64]{2,1,0:T(8,128)(2,1)S(1)} %get-tuple-element.171), channel_id=1, source_target_pairs={{0,8},{8,16},{16,24},{1,9},{9,17},{17,25},{2,10},{10,18},{18,26},{... | collective-permute-start | bytes 36872 | tf_op jit(solution)/shard_map/ppermute | solution.py:21
  26.9 14.9 %copy-start.5 = (bf16[256,512]{1,0:T(8,128)(2,1)S(1)}, bf16[256,512]{1,0:T(8,128)(2,1)}, u32[]{:S(2)}) copy-start(bf16[256,512]{1,0:T(8,128)(2,1)} %param.23) | copy-start | bytes 786436
  27.0 6.0 %collective-permute-start.7 = (bf16[4,48,128]{2,1,0:T(8,128)(2,1)S(1)}, bf16[4,48,128]{2,1,0:T(8,128)(2,1)S(1)}, u32[]{:S(2)}, u32[]{:S(2)}) collective-permute-start(bf16[4,48,128]{2,1,0:T(8,128)(2,1)S(1)} %get-tuple-element.170), channel_id=1, source_target_pairs={{8,0},{16,8},{24,16},{9,1},{17,9},{25,17},{10,2},{18,10},{26,18},{... | collective-permute-start | bytes 147464 | tf_op jit(solution)/shard_map/ppermute | solution.py:23
  28.6 5.2 %collective-permute-start.6 = (bf16[4,48,128]{2,1,0:T(8,128)(2,1)S(1)}, bf16[4,48,128]{2,1,0:T(8,128)(2,1)S(1)}, u32[]{:S(2)}, u32[]{:S(2)}) collective-permute-start(bf16[4,48,128]{2,1,0:T(8,128)(2,1)S(1)} %get-tuple-element.169), channel_id=1, source_target_pairs={{0,8},{8,16},{16,24},{1,9},{9,17},{17,25},{2,10},{10,18},{18,26},{... | collective-permute-start | bytes 147464 | tf_op jit(solution)/shard_map/ppermute | solution.py:21
  34.1 15.6 %copy-start.7 = (s32[12]{0:T(128)S(1)}, s32[12]{0:T(128)}, u32[]{:S(2)}) copy-start(s32[12]{0:T(128)} %param.17) | copy-start | bytes 148
  34.2 7.3 %collective-permute-start.9 = (bf16[8,48,256]{2,1,0:T(8,128)(2,1)S(1)}, bf16[8,48,256]{2,1,0:T(8,128)(2,1)S(1)}, u32[]{:S(2)}, u32[]{:S(2)}) collective-permute-start(bf16[8,48,256]{2,1,0:T(8,128)(2,1)S(1)} %fusion.47), channel_id=1, source_target_pairs={{8,0},{16,8},{24,16},{9,1},{17,9},{25,17},{10,2},{18,10},{26,18},{... | collective-permute-start | bytes 589832 | tf_op jit(solution)/shard_map/ppermute | solution.py:23
  35.5 6.3 %collective-permute-start.8 = (bf16[8,48,256]{2,1,0:T(8,128)(2,1)S(1)}, bf16[8,48,256]{2,1,0:T(8,128)(2,1)}, u32[]{:S(2)}, u32[]{:S(2)}) collective-permute-start(bf16[8,48,256]{2,1,0:T(8,128)(2,1)S(1)} %fusion.47), channel_id=1, source_target_pairs={{0,8},{8,16},{16,24},{1,9},{9,17},{17,25},{2,10},{10,18},{18,26},{... | collective-permute-start | bytes 589832 | tf_op jit(solution)/shard_map/ppermute | solution.py:21
  41.5 18.1 %copy-start.4 = (f32[512]{0:T(512)S(1)}, f32[512]{0:T(512)}, u32[]{:S(2)}) copy-start(f32[512]{0:T(512)} %param.24) | copy-start | bytes 6148
  43.9 15.1 %all-to-all-start = ((bf16[8,48,512]{2,1,0:T(8,128)(2,1)}), bf16[8,48,512]{2,1,0:T(8,128)(2,1)S(1)}, u32[]{:S(2)}, u32[]{:S(2)}) async-start(bf16[8,48,512]{2,1,0:T(8,128)(2,1)} %convolution_convert_fusion.2), calls=%async_computation | async-start | bytes 786432 | tf_op jit(solution)/shard_map/all_to_all | solution.py:150
  84.3 1.9 %copy-start.6 = (f32[512]{0:T(512)S(1)}, f32[512]{0:T(512)}, u32[]{:S(2)}) copy-start(f32[512]{0:T(512)} %param.27) | copy-start | bytes 6148
where the time goes:
time: 118 us; the launch traced here: 116 us
  starting transfers between devices  34.3 us (29%)
  matrix products  33.1 us (28%)
  blocking collectives  19.2 us (16%)
  waiting for transfers between devices  14.2 us (12%)
  local copies, waits for them, and re-layouts  8.62 us (7%)
  other arithmetic  6.6 us (6%)
    ppermute x5, starting transfers between devices, extended_2(): lax.ppermute(tail, axis, [(i, (i + 1) % count) for i in range(ends)])  21.7 us
    all_to_all x1, blocking collectives, per_device(): lax.all_to_all(result, 'chan', split_axis=1, concat_axis=0, tiled=True)  19.2 us
    dot_general x8, matrix products, one_block(): jnp.dot(weights, values_head, preferred_element_type=jnp.float32)  13.3 us
    all_to_all x1, waiting for transfers between devices, per_device(): lax.all_to_all(embedded, 'chan', split_axis=0, concat_axis=1, tiled=True)  9.17 us
    ppermute x5, starting transfers between devices, extended_2(): lax.ppermute(head, axis, [((i + 1) % count, i) for i in range(ends)])  6.72 us
    all_to_all x1, starting transfers between devices, per_device(): lax.all_to_all(embedded, 'chan', split_axis=0, concat_axis=1, tiled=True)  5.83 us
    dot_general x11, matrix products, dilated(): jnp.einsum('fci,io->fco', window, weight[offset], preferred_element_type=...  5.04 us
    dot_general x1, matrix products, encoder(): jnp.dot(inner, down_weight, preferred_element_type=jnp.float32)  4.41 us
  transfers between devices with their start and end apart: 11, of which 5 were waited for; matrix products, arithmetic and copies ran while one was open for 3% of the time, Pallas kernels for 0%

commit v1 on v0

--- a/solution.py
+++ b/solution.py
@@ -8,6 +8,18 @@
 STRIDE = 4
 EPSILON = 1e-05
 DILATIONS = (1, 2, 4, 8)
+
+
+def _trace_classes(inputs):
+    return jnp.concatenate(
+        lax.all_to_all(
+            jnp.stack(jnp.split(inputs, lax.axis_size("chan"), axis=0)),
+            axis_name="chan",
+            split_axis=0,
+            concat_axis=0,
+        ),
+        axis=1,
+    )
 
 
 def extended_2(cells, sides, width):
@@ -147,7 +159,7 @@
         extended = extended_2(hidden, (("tm", 0),), dilation)
         hidden = dilated(extended, weight, dilation, frames)
     embedded = project_rows(hidden, embed_weight)
-    embedded = lax.all_to_all(embedded, "chan", split_axis=0, concat_axis=1, tiled=True)
+    embedded = _trace_classes(embedded)
     all_ids = jnp.arange(channel_total, dtype=jnp.int32)
     alive_mask = jnp.logical_not(jnp.any(all_ids[:, None] == dead_channels[None, :], axis=1))
 

time: 118 us -> 122 us (1.034)
  local copies, waits for them, and re-layouts: 8.62 us -> 13.6 us
    unnamed x20 -> x27, local copies, waits for them, and re-layouts: 2.01 us -> 6.33 us
where the time goes in v1:
time: 122 us; the launch traced here: 121 us
  starting transfers between devices  34.2 us (28%)
  matrix products  32.4 us (27%)
  blocking collectives  19.2 us (16%)
  waiting for transfers between devices  14.2 us (12%)
  local copies, waits for them, and re-layouts  13.6 us (11%)
  other arithmetic  6.6 us (5%)
    ppermute x5, starting transfers between devices, extended_2(): lax.ppermute(tail, axis, [(i, (i + 1) % count) for i in range(ends)])  21.7 us
    all_to_all x1, blocking collectives, per_device(): lax.all_to_all(result, 'chan', split_axis=1, concat_axis=0, tiled=True)  19.2 us
    dot_general x8, matrix products, one_block(): jnp.dot(weights, values_head, preferred_element_type=jnp.float32)  13.3 us
    all_to_all x1, waiting for transfers between devices, _trace_classes(): lax.all_to_all(jnp.stack(jnp.split(inputs, lax.axis_size('chan'), axis=0)...  9.17 us
    ppermute x5, starting transfers between devices, extended_2(): lax.ppermute(head, axis, [((i + 1) % count, i) for i in range(ends)])  6.72 us
    unnamed x27, local copies, waits for them, and re-layouts  6.33 us
    all_to_all x1, starting transfers between devices, _trace_classes(): lax.all_to_all(jnp.stack(jnp.split(inputs, lax.axis_size('chan'), axis=0)...  5.83 us
    dot_general x11, matrix products, dilated(): jnp.einsum('fci,io->fco', window, weight[offset], preferred_element_type=...  5.04 us
  transfers between devices with their start and end apart: 11, of which 5 were waited for; matrix products, arithmetic and copies ran while one was open for 3% of the time, Pallas kernels for 0%

profile of v1, /device:TPU:0, one launch (start us, length us, event | category | flops | bytes accessed | tf_op | source)
XLA Modules:
  0.0 120.7 jit_solution(15530693608249716825)
XLA Ops:
  1.6 2.4 %collective-permute-start = (bf16[48,2]{0,1:T(2,128)(2,1)S(1)}, bf16[48,2]{0,1:T(2,128)(2,1)S(1)}, u32[]{:S(2)}, u32[]{:S(2)}) collective-permute-start(bf16[48,2]{0,1:T(2,128)(2,1)S(1)} %get-tuple-element.175), channel_id=1, source_target_pairs={{0,8},{8,16},{16,24},{1,9},{9,17},{17,25},{2,10},{10,18},{18,26},{... | collective-permute-start | bytes 584 | tf_op jit(solution)/shard_map/ppermute | solution.py:33
  4.0 1.3 %collective-permute-start.1 = (bf16[48,2]{0,1:T(2,128)(2,1)S(1)}, bf16[48,2]{0,1:T(2,128)(2,1)S(1)}, u32[]{:S(2)}, u32[]{:S(2)}) collective-permute-start(bf16[48,2]{0,1:T(2,128)(2,1)S(1)} %get-tuple-element.176), channel_id=1, source_target_pairs={{8,0},{16,8},{24,16},{9,1},{17,9},{25,17},{10,2},{18,10},{26,18},{... | collective-permute-start | bytes 584 | tf_op jit(solution)/shard_map/ppermute | solution.py:35
  5.5 3.7 %collective-permute-done.1 = bf16[48,2]{0,1:T(2,128)(2,1)S(1)} collective-permute-done((bf16[48,2]{0,1:T(2,128)(2,1)S(1)}, bf16[48,2]{0,1:T(2,128)(2,1)S(1)}, u32[]{:S(2)}, u32[]{:S(2)}) %collective-permute-start.1) | collective-permute-done | bytes 224 | tf_op jit(solution)/shard_map/ppermute | solution.py:35
  10.3 1.3 %collective-permute-start.3 = (bf16[1,48,32]{1,2,0:T(8,128)(2,1)S(1)}, bf16[1,48,32]{1,2,0:T(8,128)(2,1)S(1)}, u32[]{:S(2)}, u32[]{:S(2)}) collective-permute-start(bf16[1,48,32]{1,2,0:T(8,128)(2,1)S(1)} %get-tuple-element.174), channel_id=1, source_target_pairs={{8,0},{16,8},{24,16},{9,1},{17,9},{25,17},{10,2},{18,10},{26,18},{... | collective-permute-start | bytes 9224 | tf_op jit(solution)/shard_map/ppermute | solution.py:35
  11.6 4.9 %collective-permute-start.2 = (bf16[1,48,32]{1,2,0:T(8,128)(2,1)S(1)}, bf16[1,48,32]{1,2,0:T(8,128)(2,1)S(1)}, u32[]{:S(2)}, u32[]{:S(2)}) collective-permute-start(bf16[1,48,32]{1,2,0:T(8,128)(2,1)S(1)} %get-tuple-element.173), channel_id=1, source_target_pairs={{0,8},{8,16},{16,24},{1,9},{9,17},{17,25},{2,10},{10,18},{18,26},{... | collective-permute-start | bytes 9224 | tf_op jit(solution)/shard_map/ppermute | solution.py:33
  18.3 1.0 fusion.71
  19.3 1.4 %collective-permute-start.5 = (bf16[2,48,64]{2,1,0:T(8,128)(2,1)S(1)}, bf16[2,48,64]{2,1,0:T(8,128)(2,1)S(1)}, u32[]{:S(2)}, u32[]{:S(2)}) collective-permute-start(bf16[2,48,64]{2,1,0:T(8,128)(2,1)S(1)} %get-tuple-element.172), channel_id=1, source_target_pairs={{8,0},{16,8},{24,16},{9,1},{17,9},{25,17},{10,2},{18,10},{26,18},{... | collective-permute-start | bytes 36872 | tf_op jit(solution)/shard_map/ppermute | solution.py:35
  21.6 4.3 %collective-permute-start.4 = (bf16[2,48,64]{2,1,0:T(8,128)(2,1)S(1)}, bf16[2,48,64]{2,1,0:T(8,128)(2,1)S(1)}, u32[]{:S(2)}, u32[]{:S(2)}) collective-permute-start(bf16[2,48,64]{2,1,0:T(8,128)(2,1)S(1)} %get-tuple-element.171), channel_id=1, source_target_pairs={{0,8},{8,16},{16,24},{1,9},{9,17},{17,25},{2,10},{10,18},{18,26},{... | collective-permute-start | bytes 36872 | tf_op jit(solution)/shard_map/ppermute | solution.py:33
  27.0 1.4 %collective-permute-start.7 = (bf16[4,48,128]{2,1,0:T(8,128)(2,1)S(1)}, bf16[4,48,128]{2,1,0:T(8,128)(2,1)S(1)}, u32[]{:S(2)}, u32[]{:S(2)}) collective-permute-start(bf16[4,48,128]{2,1,0:T(8,128)(2,1)S(1)} %get-tuple-element.170), channel_id=1, source_target_pairs={{8,0},{16,8},{24,16},{9,1},{17,9},{25,17},{10,2},{18,10},{26,18},{... | collective-permute-start | bytes 147464 | tf_op jit(solution)/shard_map/ppermute | solution.py:35
  28.6 4.4 %collective-permute-start.6 = (bf16[4,48,128]{2,1,0:T(8,128)(2,1)S(1)}, bf16[4,48,128]{2,1,0:T(8,128)(2,1)S(1)}, u32[]{:S(2)}, u32[]{:S(2)}) collective-permute-start(bf16[4,48,128]{2,1,0:T(8,128)(2,1)S(1)} %get-tuple-element.169), channel_id=1, source_target_pairs={{0,8},{8,16},{16,24},{1,9},{9,17},{17,25},{2,10},{10,18},{18,26},{... | collective-permute-start | bytes 147464 | tf_op jit(solution)/shard_map/ppermute | solution.py:33
  34.1 1.3 %collective-permute-start.9 = (bf16[8,48,256]{2,1,0:T(8,128)(2,1)S(1)}, bf16[8,48,256]{2,1,0:T(8,128)(2,1)S(1)}, u32[]{:S(2)}, u32[]{:S(2)}) collective-permute-start(bf16[8,48,256]{2,1,0:T(8,128)(2,1)S(1)} %fusion.47), channel_id=1, source_target_pairs={{8,0},{16,8},{24,16},{9,1},{17,9},{25,17},{10,2},{18,10},{26,18},{... | collective-permute-start | bytes 589832 | tf_op jit(solution)/shard_map/ppermute | solution.py:35
  35.4 5.8 %collective-permute-start.8 = (bf16[8,48,256]{2,1,0:T(8,128)(2,1)S(1)}, bf16[8,48,256]{2,1,0:T(8,128)(2,1)}, u32[]{:S(2)}, u32[]{:S(2)}) collective-permute-start(bf16[8,48,256]{2,1,0:T(8,128)(2,1)S(1)} %fusion.47), channel_id=1, source_target_pairs={{0,8},{8,16},{16,24},{1,9},{9,17},{17,25},{2,10},{10,18},{18,26},{... | collective-permute-start | bytes 589832 | tf_op jit(solution)/shard_map/ppermute | solution.py:33
  41.8 1.5 %convolution_convert_fusion.2 = bf16[8,48,512]{2,1,0:T(8,128)(2,1)S(1)} fusion(f32[8,48,256]{2,1,0:T(8,128)S(1)} %fusion.99, f32[8,48,256]{2,1,0:T(8,128)S(1)} %fusion.101, bf16[8,48,256]{2,1,0:T(8,128)(2,1)} %collective-permute-done.8, bf16[256,512]{1,0:T(8,128)(2,1)S(1)} %copy-done.5, bf16[3,256,256]{2,1,0:T(8,128)(2,1)} %param.22), kind=kOutput, calls=%fused_computation.32 | convolution fusion | flops 152272896 | bytes 1769472 | tf_op jit(solution)/shard_map/fci,io->fco/dot_general | solution.py:126
  48.2 5.8 %all-to-all-start = ((bf16[8,1,48,512]{3,2,1,0:T(8,128)(2,1)}), bf16[8,1,48,512]{3,2,1,0:T(8,128)(2,1)S(1)}, u32[]{:S(2)}, u32[]{:S(2)}) async-start(bf16[8,1,48,512]{3,2,1,0:T(8,128)(2,1)} %fusion.130), calls=%async_computation | async-start | bytes 786432 | tf_op jit(solution)/shard_map/all_to_all | solution.py:15
  54.1 9.2 %all-to-all-done = bf16[8,1,48,512]{3,2,1,0:T(8,128)(2,1)S(1)} async-done(((bf16[8,1,48,512]{3,2,1,0:T(8,128)(2,1)}), bf16[8,1,48,512]{3,2,1,0:T(8,128)(2,1)S(1)}, u32[]{:S(2)}, u32[]{:S(2)}) %all-to-all-start) | async-done | bytes 393248 | tf_op jit(solution)/shard_map/all_to_all | solution.py:15
  64.1 3.2 %convolution_convert_fusion.1 = bf16[384,1536]{1,0:T(8,128)(2,1)} fusion(bf16[384,512]{1,0:T(8,128)(2,1)S(1)} %fusion.39, bf16[512,1536]{1,0:T(8,128)(2,1)} %param.25), kind=kOutput, calls=%fused_computation.25 | convolution fusion | flops 604569600 | bytes 3145728 | tf_op jit(solution)/shard_map/while/body/eval_jaxpr/dot_general | solution.py:87
  67.3 2.4 %copy.148 = bf16[384,1536]{0,1:T(8,128)(2,1)} copy(bf16[384,1536]{1,0:T(8,128)(2,1)} %convolution_convert_fusion.1) | data formatting | bytes 2359296 | tf_op jit(solution)/shard_map/while/body/eval_jaxpr/convert_element_type | solution.py:87
  69.7 2.1 %slice_bitcast_fusion = (bf16[8,384,64]{1,2,0:T(8,128)(2,1)}, bf16[8,384,64]{1,2,0:T(8,128)(2,1)S(1)}, bf16[8,384,64]{1,2,0:T(8,128)(2,1)S(1)}) fusion(bf16[384,3,8,64]{0,3,2,1:T(8,128)(2,1)} %bitcast.175), kind=kLoop, calls=%fused_computation.70 | loop fusion | bytes 2359296 | tf_op jit(solution)/shard_map/while/body/eval_jaxpr/transpose | solution.py:76
  71.8 16.7 %while.17 = (s32[]{:T(128)}, bf16[8,384,64]{1,2,0:T(8,128)(2,1)}, pred[384]{0:T(512)(128)(4,1)S(1)}, bf16[8,384,64]{1,2,0:T(8,128)(2,1)S(1)}, bf16[8,384,64]{1,2...) while((s32[]{:T(128)}, bf16[8,384,64]{1,2,0:T(8,128)(2,1)}, pred[384]{0:T(512)(128)(4,1)S(1)}, ...), condition=%wide.region_7.8_spmd, body=%wide.region_4.7_spmd.sunk | while | flops 38952192 | bytes 1976397 | solution.py:71
  72.2 1.7 %fusion.194 = bf16[8,384,64]{1,2,0:T(8,128)(2,1)} fusion(bf16[8,384,64]{1,2,0:T(8,128)(2,1)} %get-tuple-element.228, s32[]{:T(128)} %get-tuple-element.227, f32[384,384]{0,1:T(8,128)S(1)} %get-tuple-element.218, f32[384]{0:T(512)S(1)} %fusion.193, f32[384]{0:T(512)S(1)} %get-tuple-element.219, bf16[8,384,64]{1,2,0:T(8,128)(2,1)} %get-tuple-element.239), kind=kOutput, calls=%fused_computation.4.clone.1 | convolution fusion | flops 19341312 | bytes 692224 | tf_op jit(solution)/shard_map/while/body/eval_jaxpr/while/body/eval_jaxpr/while/body/eval_jaxpr/dot_general | solution.py:65
  74.3 1.7 %fusion.194 = bf16[8,384,64]{1,2,0:T(8,128)(2,1)} fusion(bf16[8,384,64]{1,2,0:T(8,128)(2,1)} %get-tuple-element.228, s32[]{:T(128)} %get-tuple-element.227, f32[384,384]{0,1:T(8,128)S(1)} %get-tuple-element.218, f32[384]{0:T(512)S(1)} %fusion.193, f32[384]{0:T(512)S(1)} %get-tuple-element.219, bf16[8,384,64]{1,2,0:T(8,128)(2,1)} %get-tuple-element.239), kind=kOutput, calls=%fused_computation.4.clone.1 | convolution fusion | flops 19341312 | bytes 692224 | tf_op jit(solution)/shard_map/while/body/eval_jaxpr/while/body/eval_jaxpr/while/body/eval_jaxpr/dot_general | solution.py:65
  76.4 1.7 %fusion.194 = bf16[8,384,64]{1,2,0:T(8,128)(2,1)} fusion(bf16[8,384,64]{1,2,0:T(8,128)(2,1)} %get-tuple-element.228, s32[]{:T(128)} %get-tuple-element.227, f32[384,384]{0,1:T(8,128)S(1)} %get-tuple-element.218, f32[384]{0:T(512)S(1)} %fusion.193, f32[384]{0:T(512)S(1)} %get-tuple-element.219, bf16[8,384,64]{1,2,0:T(8,128)(2,1)} %get-tuple-element.239), kind=kOutput, calls=%fused_computation.4.clone.1 | convolution fusion | flops 19341312 | bytes 692224 | tf_op jit(solution)/shard_map/while/body/eval_jaxpr/while/body/eval_jaxpr/while/body/eval_jaxpr/dot_general | solution.py:65
  78.5 1.7 %fusion.194 = bf16[8,384,64]{1,2,0:T(8,128)(2,1)} fusion(bf16[8,384,64]{1,2,0:T(8,128)(2,1)} %get-tuple-element.228, s32[]{:T(128)} %get-tuple-element.227, f32[384,384]{0,1:T(8,128)S(1)} %get-tuple-element.218, f32[384]{0:T(512)S(1)} %fusion.193, f32[384]{0:T(512)S(1)} %get-tuple-element.219, bf16[8,384,64]{1,2,0:T(8,128)(2,1)} %get-tuple-element.239), kind=kOutput, calls=%fused_computation.4.clone.1 | convolution fusion | flops 19341312 | bytes 692224 | tf_op jit(solution)/shard_map/while/body/eval_jaxpr/while/body/eval_jaxpr/while/body/eval_jaxpr/dot_general | solution.py:65
  80.6 1.7 %fusion.194 = bf16[8,384,64]{1,2,0:T(8,128)(2,1)} fusion(bf16[8,384,64]{1,2,0:T(8,128)(2,1)} %get-tuple-element.228, s32[]{:T(128)} %get-tuple-element.227, f32[384,384]{0,1:T(8,128)S(1)} %get-tuple-element.218, f32[384]{0:T(512)S(1)} %fusion.193, f32[384]{0:T(512)S(1)} %get-tuple-element.219, bf16[8,384,64]{1,2,0:T(8,128)(2,1)} %get-tuple-element.239), kind=kOutput, calls=%fused_computation.4.clone.1 | convolution fusion | flops 19341312 | bytes 692224 | tf_op jit(solution)/shard_map/while/body/eval_jaxpr/while/body/eval_jaxpr/while/body/eval_jaxpr/dot_general | solution.py:65
  82.7 1.7 %fusion.194 = bf16[8,384,64]{1,2,0:T(8,128)(2,1)} fusion(bf16[8,384,64]{1,2,0:T(8,128)(2,1)} %get-tuple-element.228, s32[]{:T(128)} %get-tuple-element.227, f32[384,384]{0,1:T(8,128)S(1)} %get-tuple-element.218, f32[384]{0:T(512)S(1)} %fusion.193, f32[384]{0:T(512)S(1)} %get-tuple-element.219, bf16[8,384,64]{1,2,0:T(8,128)(2,1)} %get-tuple-element.239), kind=kOutput, calls=%fused_computation.4.clone.1 | convolution fusion | flops 19341312 | bytes 692224 | tf_op jit(solution)/shard_map/while/body/eval_jaxpr/while/body/eval_jaxpr/while/body/eval_jaxpr/dot_general | solution.py:65
  84.8 1.7 %fusion.194 = bf16[8,384,64]{1,2,0:T(8,128)(2,1)} fusion(bf16[8,384,64]{1,2,0:T(8,128)(2,1)} %get-tuple-element.228, s32[]{:T(128)} %get-tuple-element.227, f32[384,384]{0,1:T(8,128)S(1)} %get-tuple-element.218, f32[384]{0:T(512)S(1)} %fusion.193, f32[384]{0:T(512)S(1)} %get-tuple-element.219, bf16[8,384,64]{1,2,0:T(8,128)(2,1)} %get-tuple-element.239), kind=kOutput, calls=%fused_computation.4.clone.1 | convolution fusion | flops 19341312 | bytes 692224 | tf_op jit(solution)/shard_map/while/body/eval_jaxpr/while/body/eval_jaxpr/while/body/eval_jaxpr/dot_general | solution.py:65
  86.9 1.7 %fusion.194 = bf16[8,384,64]{1,2,0:T(8,128)(2,1)} fusion(bf16[8,384,64]{1,2,0:T(8,128)(2,1)} %get-tuple-element.228, s32[]{:T(128)} %get-tuple-element.227, f32[384,384]{0,1:T(8,128)S(1)} %get-tuple-element.218, f32[384]{0:T(512)S(1)} %fusion.193, f32[384]{0:T(512)S(1)} %get-tuple-element.219, bf16[8,384,64]{1,2,0:T(8,128)(2,1)} %get-tuple-element.239), kind=kOutput, calls=%fused_computation.4.clone.1 | convolution fusion | flops 19341312 | bytes 692224 | tf_op jit(solution)/shard_map/while/body/eval_jaxpr/while/body/eval_jaxpr/while/body/eval_jaxpr/dot_general | solution.py:65
  88.5 1.7 %fusion.173 = (f32[384]{0:T(512)S(1)}, f32[384,512]{1,0:T(8,128)S(1)}) fusion(bf16[384,512]{0,1:T(8,128)(2,1)} %bitcast.178, bf16[512,512]{1,0:T(8,128)(2,1)} %param.26, bf16[384,512]{1,0:T(8,128)(2,1)S(1)} %bitcast.174), kind=kOutput, calls=%fused_computation.204 | convolution fusion | flops 202309248 | bytes 2098688 | tf_op jit(solution)/shard_map/while/body/eval_jaxpr/dot_general | solution.py:92
  90.5 4.4 %fusion.30 = bf16[1,384,512]{2,1,0:T(8,128)(2,1)} fusion(f32[384,512]{1,0:T(8,128)S(1)} %get-tuple-element.178, bf16[2048,512]{1,0:T(8,128)(2,1)S(1)} %copy-done, bf16[512,2048]{1,0:T(8,128)(2,1)} %param.28, f32[512]{0:T(512)S(1)} %copy-done.6, f32[384]{0:T(512)S(1)} %add_rsqrt_fusion.1, f32[384]{0:T(512)S(1)} %broadcast_multiply_fusion.1), kind=kOutput, calls=%fused_computation.33 | convolution fusion | flops 1618870272 | bytes 5379072 | tf_op jit(solution)/shard_map/while/body/eval_jaxpr/dot_general | solution.py:99
  94.9 1.6 %copy.158 = bf16[1,384,512]{2,0,1:T(2,128)(2,1)S(1)} copy(bf16[1,384,512]{2,1,0:T(8,128)(2,1)} %fusion.30) | data formatting | bytes 786432 | tf_op jit(solution)/shard_map/while/body/jit(dynamic_update_index_in_dim)/broadcast_in_dim | solution.py:178
  97.0 3.0 %reduce.4 = bf16[384,512]{1,0:T(8,128)(2,1)S(1)} reduce(bf16[384,1,512]{2,1,0:T(2,128)(2,1)S(1)} %bitcast.176, bf16[]{:T(256)} %broadcast.174), dimensions={1}, to_apply=%bitcast.165.reduce_sub_computation | reduce | bytes 786434
  100.3 19.2 %all_to_all.17 = bf16[8,2,12288]{2,1,0:T(2,128)(2,1)S(1)} all-to-all(bf16[8,2,12288]{2,1,0:T(2,128)(2,1)S(1)} %reshape.97), channel_id=1, replica_groups=mesh['tm'=4,'chan'=8] {'chan'}, dimensions={0} | all-to-all | bytes 786432 | tf_op jit(solution)/shard_map/all_to_all | solution.py:179
  (103 shorter events, 19.9 us)
Async XLA Ops:
  0.0 90.4 %copy-start = (bf16[2048,512]{1,0:T(8,128)(2,1)S(1)}, bf16[2048,512]{1,0:T(8,128)(2,1)}, u32[]{:S(2)}) copy-start(bf16[2048,512]{1,0:T(8,128)(2,1)} %param.29) | copy-start | bytes 6291460
  0.0 25.9 %copy-start.3 = (bf16[3,64,128]{2,1,0:T(8,128)(2,1)S(1)}, bf16[3,64,128]{2,1,0:T(8,128)(2,1)}, u32[]{:S(2)}) copy-start(bf16[3,64,128]{2,1,0:T(8,128)(2,1)} %param.20) | copy-start | bytes 147460
  0.0 28.4 %copy-start.2 = (bf16[3,128,256]{2,1,0:T(8,128)(2,1)S(1)}, bf16[3,128,256]{2,1,0:T(8,128)(2,1)}, u32[]{:S(2)}) copy-start(bf16[3,128,256]{2,1,0:T(8,128)(2,1)} %param.21) | copy-start | bytes 589828
  1.6 3.8 %collective-permute-start = (bf16[48,2]{0,1:T(2,128)(2,1)S(1)}, bf16[48,2]{0,1:T(2,128)(2,1)S(1)}, u32[]{:S(2)}, u32[]{:S(2)}) collective-permute-start(bf16[48,2]{0,1:T(2,128)(2,1)S(1)} %get-tuple-element.175), channel_id=1, source_target_pairs={{0,8},{8,16},{16,24},{1,9},{9,17},{17,25},{2,10},{10,18},{18,26},{... | collective-permute-start | bytes 584 | tf_op jit(solution)/shard_map/ppermute | solution.py:33
  4.0 5.1 %collective-permute-start.1 = (bf16[48,2]{0,1:T(2,128)(2,1)S(1)}, bf16[48,2]{0,1:T(2,128)(2,1)S(1)}, u32[]{:S(2)}, u32[]{:S(2)}) collective-permute-start(bf16[48,2]{0,1:T(2,128)(2,1)S(1)} %get-tuple-element.176), channel_id=1, source_target_pairs={{8,0},{16,8},{24,16},{9,1},{17,9},{25,17},{10,2},{18,10},{26,18},{... | collective-permute-start | bytes 584 | tf_op jit(solution)/shard_map/ppermute | solution.py:35
  10.3 7.1 %collective-permute-start.3 = (bf16[1,48,32]{1,2,0:T(8,128)(2,1)S(1)}, bf16[1,48,32]{1,2,0:T(8,128)(2,1)S(1)}, u32[]{:S(2)}, u32[]{:S(2)}) collective-permute-start(bf16[1,48,32]{1,2,0:T(8,128)(2,1)S(1)} %get-tuple-element.174), channel_id=1, source_target_pairs={{8,0},{16,8},{24,16},{9,1},{17,9},{25,17},{10,2},{18,10},{26,18},{... | collective-permute-start | bytes 9224 | tf_op jit(solution)/shard_map/ppermute | solution.py:35
  11.6 6.7 %collective-permute-start.2 = (bf16[1,48,32]{1,2,0:T(8,128)(2,1)S(1)}, bf16[1,48,32]{1,2,0:T(8,128)(2,1)S(1)}, u32[]{:S(2)}, u32[]{:S(2)}) collective-permute-start(bf16[1,48,32]{1,2,0:T(8,128)(2,1)S(1)} %get-tuple-element.173), channel_id=1, source_target_pairs={{0,8},{8,16},{16,24},{1,9},{9,17},{17,25},{2,10},{10,18},{18,26},{... | collective-permute-start | bytes 9224 | tf_op jit(solution)/shard_map/ppermute | solution.py:33
  19.3 22.0 %copy-start.1 = (bf16[3,256,256]{2,1,0:T(8,128)(2,1)S(1)}, bf16[3,256,256]{2,1,0:T(8,128)(2,1)}, u32[]{:S(2)}) copy-start(bf16[3,256,256]{2,1,0:T(8,128)(2,1)} %param.22) | copy-start | bytes 1179652
  19.3 6.6 %collective-permute-start.5 = (bf16[2,48,64]{2,1,0:T(8,128)(2,1)S(1)}, bf16[2,48,64]{2,1,0:T(8,128)(2,1)S(1)}, u32[]{:S(2)}, u32[]{:S(2)}) collective-permute-start(bf16[2,48,64]{2,1,0:T(8,128)(2,1)S(1)} %get-tuple-element.172), channel_id=1, source_target_pairs={{8,0},{16,8},{24,16},{9,1},{17,9},{25,17},{10,2},{18,10},{26,18},{... | collective-permute-start | bytes 36872 | tf_op jit(solution)/shard_map/ppermute | solution.py:35
  21.6 5.1 %collective-permute-start.4 = (bf16[2,48,64]{2,1,0:T(8,128)(2,1)S(1)}, bf16[2,48,64]{2,1,0:T(8,128)(2,1)S(1)}, u32[]{:S(2)}, u32[]{:S(2)}) collective-permute-start(bf16[2,48,64]{2,1,0:T(8,128)(2,1)S(1)} %get-tuple-element.171), channel_id=1, source_target_pairs={{0,8},{8,16},{16,24},{1,9},{9,17},{17,25},{2,10},{10,18},{18,26},{... | collective-permute-start | bytes 36872 | tf_op jit(solution)/shard_map/ppermute | solution.py:33
  26.9 14.8 %copy-start.5 = (bf16[256,512]{1,0:T(8,128)(2,1)S(1)}, bf16[256,512]{1,0:T(8,128)(2,1)}, u32[]{:S(2)}) copy-start(bf16[256,512]{1,0:T(8,128)(2,1)} %param.23) | copy-start | bytes 786436
  27.0 6.0 %collective-permute-start.7 = (bf16[4,48,128]{2,1,0:T(8,128)(2,1)S(1)}, bf16[4,48,128]{2,1,0:T(8,128)(2,1)S(1)}, u32[]{:S(2)}, u32[]{:S(2)}) collective-permute-start(bf16[4,48,128]{2,1,0:T(8,128)(2,1)S(1)} %get-tuple-element.170), channel_id=1, source_target_pairs={{8,0},{16,8},{24,16},{9,1},{17,9},{25,17},{10,2},{18,10},{26,18},{... | collective-permute-start | bytes 147464 | tf_op jit(solution)/shard_map/ppermute | solution.py:35
  28.6 5.2 %collective-permute-start.6 = (bf16[4,48,128]{2,1,0:T(8,128)(2,1)S(1)}, bf16[4,48,128]{2,1,0:T(8,128)(2,1)S(1)}, u32[]{:S(2)}, u32[]{:S(2)}) collective-permute-start(bf16[4,48,128]{2,1,0:T(8,128)(2,1)S(1)} %get-tuple-element.169), channel_id=1, source_target_pairs={{0,8},{8,16},{16,24},{1,9},{9,17},{17,25},{2,10},{10,18},{18,26},{... | collective-permute-start | bytes 147464 | tf_op jit(solution)/shard_map/ppermute | solution.py:33
  34.1 7.3 %collective-permute-start.9 = (bf16[8,48,256]{2,1,0:T(8,128)(2,1)S(1)}, bf16[8,48,256]{2,1,0:T(8,128)(2,1)S(1)}, u32[]{:S(2)}, u32[]{:S(2)}) collective-permute-start(bf16[8,48,256]{2,1,0:T(8,128)(2,1)S(1)} %fusion.47), channel_id=1, source_target_pairs={{8,0},{16,8},{24,16},{9,1},{17,9},{25,17},{10,2},{18,10},{26,18},{... | collective-permute-start | bytes 589832 | tf_op jit(solution)/shard_map/ppermute | solution.py:35
  35.4 6.3 %collective-permute-start.8 = (bf16[8,48,256]{2,1,0:T(8,128)(2,1)S(1)}, bf16[8,48,256]{2,1,0:T(8,128)(2,1)}, u32[]{:S(2)}, u32[]{:S(2)}) collective-permute-start(bf16[8,48,256]{2,1,0:T(8,128)(2,1)S(1)} %fusion.47), channel_id=1, source_target_pairs={{0,8},{8,16},{16,24},{1,9},{9,17},{17,25},{2,10},{10,18},{18,26},{... | collective-permute-start | bytes 589832 | tf_op jit(solution)/shard_map/ppermute | solution.py:33
  41.5 12.5 %copy-start.7 = (s32[12]{0:T(128)S(1)}, s32[12]{0:T(128)}, u32[]{:S(2)}) copy-start(s32[12]{0:T(128)} %param.17) | copy-start | bytes 148
  41.7 22.2 %copy-start.4 = (f32[512]{0:T(512)S(1)}, f32[512]{0:T(512)}, u32[]{:S(2)}) copy-start(f32[512]{0:T(512)} %param.24) | copy-start | bytes 6148
  48.2 15.1 %all-to-all-start = ((bf16[8,1,48,512]{3,2,1,0:T(8,128)(2,1)}), bf16[8,1,48,512]{3,2,1,0:T(8,128)(2,1)S(1)}, u32[]{:S(2)}, u32[]{:S(2)}) async-start(bf16[8,1,48,512]{3,2,1,0:T(8,128)(2,1)} %fusion.130), calls=%async_computation | async-start | bytes 786432 | tf_op jit(solution)/shard_map/all_to_all | solution.py:15
  88.5 1.9 %copy-start.6 = (f32[512]{0:T(512)S(1)}, f32[512]{0:T(512)}, u32[]{:S(2)}) copy-start(f32[512]{0:T(512)} %param.27) | copy-start | bytes 6148
